TPU v7x, 128 devices: a whole 4x4x4 slice. The times are simulated.
128 devices in a mesh: row: 16 (over x, y), col: 4 (over z), layer: 2 (over core).
Axes of the slice: x: 4, y: 4, z: 4, core: 2. Of those that a mesh axis runs over, the one named last changes fastest.
Arguments:
- density: float32 [4096, 4096], P('row', ('col', 'layer')), may hold values from -2 to 2
- masks: int32 [6, 64, 64], replicated, may hold values from 0 to 1, as said below
- branch: int32 [5], replicated, may hold values from 0 to 1, as said below
- perm: int32 [64], replicated, may hold values from 0 to 63, each once
Outputs:
- purified: float32 [4096, 4096], P('row', ('col', 'layer'))
Inputs may be any that keep to these rules, and one draw needn't show every extreme that they name: masks are symmetric in their last two dimensions, every diagonal block is occupied, and block (i, j) of masks[s] is occupied only where the cyclic distance between i and j is at most 6 + s. `branch`: both values occur among the steps. `perm`: a permutation of 0..63.
All inputs are finite; a program needn't handle non-finite values.
Results may differ from a plain program's by a relative error of at most 0.0003.
Values sent between devices are 32-bit elements; how exact they have to be, the bound alone decides.
No kernel may reach another device: no remote copies, remote signals or barrier semaphores. Data moves between devices by JAX's collectives and lax.ppermute only.
A program may use at most 64 MiB of HBM per device.

v0:
```python
import jax
import jax.numpy as jnp
from jax import lax
from jax.sharding import PartitionSpec as P

BS = 64
STEPS = 5


def expand(block_mask):
    grown = jnp.repeat(block_mask, BS, axis=0)
    return jnp.repeat(grown, BS, axis=1).astype(jnp.float32)


def shards(density, masks, branch, perm):
    rows_here = density.shape[0]
    cols_here = density.shape[1]
    row_blocks = rows_here // BS
    col_blocks = cols_here // BS
    row_start = lax.axis_index("row") * row_blocks
    col_start = lax.axis_index(("col", "layer")) * col_blocks
    row_ids = lax.dynamic_slice_in_dim(perm, row_start, row_blocks)
    col_ids = lax.dynamic_slice_in_dim(perm, col_start, col_blocks)
    local_masks = jnp.take(jnp.take(masks, row_ids, axis=1), col_ids, axis=2)
    current = density * expand(local_masks[0])
    for step in range(STEPS):
        panel = lax.all_gather(current, ("col", "layer"), axis=1, tiled=True)
        square = jnp.dot(
            panel,
            lax.all_gather(current, "row", axis=0, tiled=True),
            preferred_element_type=jnp.float32,
            precision=lax.Precision.HIGHEST,
        )
        picked = jnp.where(branch[step] == 1, 2.0 * current - square, square)
        current = picked * expand(local_masks[step + 1])
    return current


def solution(mesh):
    return jax.shard_map(
        shards,
        mesh=mesh,
        in_specs=(P("row", ("col", "layer")), P(), P(), P()),
        out_specs=P("row", ("col", "layer")),
        check_vma=False,
    )
```

profile of v0, /device:TPU:1, one launch (start us, length us, event | category | flops | bytes accessed | tf_op | source)
XLA Modules:
  0.0 603.6 jit_solution(2125554987655784131)
XLA Ops:
  6.5 0.8 compare_and_fusion
  7.5 0.6 gather_fusion
  8.3 0.7 compare_and_fusion.1
  9.0 0.6 gather_fusion.1
  10.2 1.9 mul.45
  12.2 0.7 all-gather.13.cloned.1.call-update
  13.5 1.5 fusion.11
  15.5 32.8 %all-gather.11.cloned.1.call-done = f32[256,4096]{1,0:T(8,128)} async-done(((f32[256,512]{1,0:T(8,128)}), f32[256,4096]{1,0:T(8,128)}) %all-gather.11.cloned.1.call-update) | async-done | bytes 4194320 | tf_op jit(solution)/shard_map/all_gather | solution.py:27
  48.3 72.2 %all-gather.13.cloned.1.call-done = f32[4096,512]{1,0:T(8,128)} async-done(((f32[256,512]{1,0:T(8,128)}), f32[4096,512]{1,0:T(8,128)}) %all-gather.13.cloned.1.call-update) | async-done | bytes 8388624 | tf_op jit(solution)/shard_map/all_gather | solution.py:30
  120.5 11.5 %fusion = f32[256,512]{1,0:T(8,128)} fusion(f32[256,512]{1,0:T(8,128)S(1)} %copy.29, f32[256,512]{1,0:T(8,128)} %mul.45, pred[]{:T(512)} %bitcast.4, f32[256,4096]{1,0:T(8,128)} %all-gather.11.cloned.1.call-done, f32[4096,512]{1,0:T(8,128)} %all-gather.13.cloned.1.call-done), kind=kOutput, calls=%fused_computation.7 | convolution fusion | flops 6442975232 | bytes 14155777 | tf_op jit(solution)/shard_map/dot_general | solution.py:28
  132.0 0.5 all-gather.17.cloned.1.call-update
  133.8 30.8 %all-gather.15.cloned.1.call-done = f32[256,4096]{1,0:T(8,128)} async-done(((f32[256,512]{1,0:T(8,128)}), f32[256,4096]{1,0:T(8,128)}) %all-gather.15.cloned.1.call-update) | async-done | bytes 4194320 | tf_op jit(solution)/shard_map/all_gather | solution.py:27
  164.6 72.0 %all-gather.17.cloned.1.call-done = f32[4096,512]{1,0:T(8,128)} async-done(((f32[256,512]{1,0:T(8,128)}), f32[4096,512]{1,0:T(8,128)}) %all-gather.17.cloned.1.call-update) | async-done | bytes 8388624 | tf_op jit(solution)/shard_map/all_gather | solution.py:30
  236.6 11.5 %fusion.1 = f32[256,512]{1,0:T(8,128)} fusion(f32[256,512]{1,0:T(8,128)S(1)} %copy.31, f32[256,512]{1,0:T(8,128)} %fusion, pred[]{:T(512)} %bitcast.3, f32[256,4096]{1,0:T(8,128)} %all-gather.15.cloned.1.call-done, f32[4096,512]{1,0:T(8,128)} %all-gather.17.cloned.1.call-done), kind=kOutput, calls=%fused_computation.8 | convolution fusion | flops 6442975232 | bytes 14155777 | tf_op jit(solution)/shard_map/dot_general | solution.py:28
  250.1 30.7 %all-gather.19.cloned.1.call-done = f32[256,4096]{1,0:T(8,128)} async-done(((f32[256,512]{1,0:T(8,128)}), f32[256,4096]{1,0:T(8,128)}) %all-gather.19.cloned.1.call-update) | async-done | bytes 4194320 | tf_op jit(solution)/shard_map/all_gather | solution.py:27
  280.8 72.0 %all-gather.21.cloned.1.call-done = f32[4096,512]{1,0:T(8,128)} async-done(((f32[256,512]{1,0:T(8,128)}), f32[4096,512]{1,0:T(8,128)}) %all-gather.21.cloned.1.call-update) | async-done | bytes 8388624 | tf_op jit(solution)/shard_map/all_gather | solution.py:30
  352.8 11.5 %fusion.2 = f32[256,512]{1,0:T(8,128)} fusion(f32[256,512]{1,0:T(8,128)S(1)} %copy.33, f32[256,512]{1,0:T(8,128)} %fusion.1, pred[]{:T(512)} %bitcast.2, f32[256,4096]{1,0:T(8,128)} %all-gather.19.cloned.1.call-done, f32[4096,512]{1,0:T(8,128)} %all-gather.21.cloned.1.call-done), kind=kOutput, calls=%fused_computation.9 | convolution fusion | flops 6442975232 | bytes 14155777 | tf_op jit(solution)/shard_map/dot_general | solution.py:28
  364.4 0.7 all-gather.25.cloned.1.call-update
  366.2 30.7 %all-gather.23.cloned.1.call-done = f32[256,4096]{1,0:T(8,128)} async-done(((f32[256,512]{1,0:T(8,128)}), f32[256,4096]{1,0:T(8,128)}) %all-gather.23.cloned.1.call-update) | async-done | bytes 4194320 | tf_op jit(solution)/shard_map/all_gather | solution.py:27
  397.0 72.2 %all-gather.25.cloned.1.call-done = f32[4096,512]{1,0:T(8,128)} async-done(((f32[256,512]{1,0:T(8,128)}), f32[4096,512]{1,0:T(8,128)}) %all-gather.25.cloned.1.call-update) | async-done | bytes 8388624 | tf_op jit(solution)/shard_map/all_gather | solution.py:30
  469.1 11.5 %fusion.3 = f32[256,512]{1,0:T(8,128)} fusion(f32[256,512]{1,0:T(8,128)S(1)} %copy.35, f32[256,512]{1,0:T(8,128)} %fusion.2, pred[]{:T(512)} %bitcast.1, f32[256,4096]{1,0:T(8,128)} %all-gather.23.cloned.1.call-done, f32[4096,512]{1,0:T(8,128)} %all-gather.25.cloned.1.call-done), kind=kOutput, calls=%fused_computation.10 | convolution fusion | flops 6442975232 | bytes 14155777 | tf_op jit(solution)/shard_map/dot_general | solution.py:28
  482.4 30.8 %all-gather.27.cloned.1.call-done = f32[256,4096]{1,0:T(8,128)} async-done(((f32[256,512]{1,0:T(8,128)}), f32[256,4096]{1,0:T(8,128)}) %all-gather.27.cloned.1.call-update) | async-done | bytes 4194320 | tf_op jit(solution)/shard_map/all_gather | solution.py:27
  513.2 72.0 %all-gather.29.cloned.1.call-done = f32[4096,512]{1,0:T(8,128)} async-done(((f32[256,512]{1,0:T(8,128)}), f32[4096,512]{1,0:T(8,128)}) %all-gather.29.cloned.1.call-update) | async-done | bytes 8388624 | tf_op jit(solution)/shard_map/all_gather | solution.py:30
  585.3 11.5 %fusion.4 = f32[256,512]{1,0:T(8,128)} fusion(f32[256,512]{1,0:T(8,128)S(1)} %copy.37, f32[256,512]{1,0:T(8,128)} %fusion.3, pred[]{:T(512)} %bitcast, f32[256,4096]{1,0:T(8,128)} %all-gather.27.cloned.1.call-done, f32[4096,512]{1,0:T(8,128)} %all-gather.29.cloned.1.call-done), kind=kOutput, calls=%fused_computation.11 | convolution fusion | flops 6442975232 | bytes 14155777 | tf_op jit(solution)/shard_map/dot_general | solution.py:28
  (58 shorter events, 5.1 us)
Async XLA Ops:
  6.5 0.9 copy-start
  6.5 41.8 %all-gather.11.cloned.1.call-start = ((), (), s32[]{:S(2)}) async-start(), calls=%async_computation | async-start | bytes 4718592 | tf_op jit(solution)/shard_map/all_gather | solution.py:27
  12.2 108.3 %all-gather.13.cloned.1.call-start = ((), (), s32[]{:S(2)}) async-start(), calls=%async_computation.1 | async-start | bytes 8912896 | tf_op jit(solution)/shard_map/all_gather | solution.py:30
  12.9 151.7 %all-gather.15.cloned.1.call-start = ((), (), s32[]{:S(2)}) async-start(), calls=%async_computation.2 | async-start | bytes 4718592 | tf_op jit(solution)/shard_map/all_gather | solution.py:27
  132.0 104.7 %all-gather.17.cloned.1.call-start = ((), (), s32[]{:S(2)}) async-start(), calls=%async_computation.3 | async-start | bytes 8912896 | tf_op jit(solution)/shard_map/all_gather | solution.py:30
  132.6 148.2 %all-gather.19.cloned.1.call-start = ((), (), s32[]{:S(2)}) async-start(), calls=%async_computation.4 | async-start | bytes 4718592 | tf_op jit(solution)/shard_map/all_gather | solution.py:27
  248.1 104.7 %all-gather.21.cloned.1.call-start = ((), (), s32[]{:S(2)}) async-start(), calls=%async_computation.5 | async-start | bytes 8912896 | tf_op jit(solution)/shard_map/all_gather | solution.py:30
  248.7 148.3 %all-gather.23.cloned.1.call-start = ((), (), s32[]{:S(2)}) async-start(), calls=%async_computation.6 | async-start | bytes 4718592 | tf_op jit(solution)/shard_map/all_gather | solution.py:27
  364.3 104.8 %all-gather.25.cloned.1.call-start = ((), (), s32[]{:S(2)}) async-start(), calls=%async_computation.7 | async-start | bytes 8912896 | tf_op jit(solution)/shard_map/all_gather | solution.py:30
  365.1 148.2 %all-gather.27.cloned.1.call-start = ((), (), s32[]{:S(2)}) async-start(), calls=%async_computation.8 | async-start | bytes 4718592 | tf_op jit(solution)/shard_map/all_gather | solution.py:27
  480.6 116.1 %copy-start.1 = (s32[6,64,64]{2,1,0:T(8,128)S(1)}, s32[6,64,64]{2,1,0:T(8,128)}, u32[]{:S(2)}) copy-start(s32[6,64,64]{2,1,0:T(8,128)} %param.5) | copy-start | bytes 294916
  480.6 104.6 %all-gather.29.cloned.1.call-start = ((), (), s32[]{:S(2)}) async-start(), calls=%async_computation.9 | async-start | bytes 8912896 | tf_op jit(solution)/shard_map/all_gather | solution.py:30
Sparse Core Ops, SparseCore 0:
  12.3 35.9 all-gather.10
  50.5 69.9 all-gather.12
  132.1 32.4 all-gather.14
  166.6 69.9 all-gather.16
  248.3 32.5 all-gather.18
  282.8 69.9 all-gather.20
  364.4 32.4 all-gather.22
  399.1 69.9 all-gather.24
  480.7 32.4 all-gather.26
  515.2 69.9 all-gather.28
where the time goes:
time: 604 us
  waiting for transfers between devices  519 us (86%)
  matrix products  57.3 us (9%)
  between operations  16.9 us (3%)
    all_gather x5, waiting for transfers between devices, shards(): lax.all_gather(current, 'row', axis=0, tiled=True)  360 us
    all_gather x5, waiting for transfers between devices, shards(): panel = lax.all_gather(current, ('col', 'layer'), axis=1, tiled=True)  156 us
    dot_general x5, matrix products, shards(): jnp.dot(panel, lax.all_gather(current, 'row', axis=0, tiled=True), prefer...  57.3 us
  transfers between devices with their start and end apart: 10, of which 10 were waited for; matrix products, arithmetic and copies ran while one was open for 1% of the time, Pallas kernels for 0%

commit v1 on v0

--- a/solution.py
+++ b/solution.py
@@ -24,7 +24,10 @@
     local_masks = jnp.take(jnp.take(masks, row_ids, axis=1), col_ids, axis=2)
     current = density * expand(local_masks[0])
     for step in range(STEPS):
-        panel = lax.all_gather(current, ("col", "layer"), axis=1, tiled=True)
+        devices = lax.axis_size(("col", "layer"))
+        blocks = jnp.stack([current for _ in range(devices)])
+        blocks = lax.all_to_all(blocks, ("col", "layer"), split_axis=0, concat_axis=0)
+        panel = jnp.concatenate(blocks, axis=1)
         square = jnp.dot(
             panel,
             lax.all_gather(current, "row", axis=0, tiled=True),

time: 604 us -> 471 us (0.78); the launches traced: 604 us -> 463 us
  waiting for transfers between devices: 519 us -> 303 us
  matrix products: 57.3 us -> 88.5 us
  starting transfers between devices: 0.76 us -> 29.3 us
  local copies, waits for them, and re-layouts: 5.94 us -> 22.8 us
    all_gather x5, waiting for transfers between devices: 360 us -> 65.3 us  [shards(): lax.all_gather(current, 'row', axis=0, tiled=True)]
    all_to_all x0 -> x5, waiting for transfers between devices: none -> 237 us  [shards(): lax.all_to_all(blocks, ('col', 'layer'), split_axis=0, concat_axis=0)]
    all_gather x5 -> x0, waiting for transfers between devices: 156 us -> none  [shards(): panel = lax.all_gather(current, ('col', 'layer'), axis=1, tiled=True)]
    dot_general x5, matrix products: 57.3 us -> 88.5 us  [shards(): jnp.dot(panel, lax.all_gather(current, 'row', axis=0, tiled=True), prefer...]
    all_to_all x0 -> x5, starting transfers between devices: none -> 28.3 us  [shards(): lax.all_to_all(blocks, ('col', 'layer'), split_axis=0, concat_axis=0)]
    another operation x0 -> x5, local copies, waits for them, and re-layouts: none -> 11.4 us  [shards(): blocks = jnp.stack([current for _ in range(devices)])]
    mul x0 -> x5, local copies, waits for them, and re-layouts: none -> 6.19 us  [the longest x4 4.96 us: shards(): current = picked * expand(local_masks[step + 1])]
  transfers between devices with their start and end apart: 10 -> 10, of which waited for: 10 -> 10; matrix products, arithmetic and copies ran while one was open for 1% -> 4% of each run, Pallas kernels for 0% -> 0%
where the time goes in v1:
time: 471 us; the launch traced here: 463 us
  waiting for transfers between devices  303 us (64%)
  matrix products  88.5 us (19%)
  starting transfers between devices  29.3 us (6%)
  local copies, waits for them, and re-layouts  22.8 us (5%)
  between operations  16.7 us (4%)
    all_to_all x5, waiting for transfers between devices, shards(): lax.all_to_all(blocks, ('col', 'layer'), split_axis=0, concat_axis=0)  237 us
    dot_general x5, matrix products, shards(): jnp.dot(panel, lax.all_gather(current, 'row', axis=0, tiled=True), prefer...  88.5 us
    all_gather x5, waiting for transfers between devices, shards(): lax.all_gather(current, 'row', axis=0, tiled=True)  65.3 us
    all_to_all x5, starting transfers between devices, shards(): lax.all_to_all(blocks, ('col', 'layer'), split_axis=0, concat_axis=0)  28.3 us
    another operation x5, local copies, waits for them, and re-layouts, shards(): blocks = jnp.stack([current for _ in range(devices)])  11.4 us
  transfers between devices with their start and end apart: 10, of which 10 were waited for; matrix products, arithmetic and copies ran while one was open for 4% of the time, Pallas kernels for 0%

profile of v1, /device:TPU:1, one launch (start us, length us, event | category | flops | bytes accessed | tf_op | source)
XLA Modules:
  0.0 463.5 jit_solution(10956111079362212845)
XLA Ops:
  13.4 2.3 stack.10
  15.7 6.9 %all-to-all-start = ((f32[8,256,512]{1,2,0:T(8,128)}), f32[8,256,512]{1,2,0:T(8,128)}, u32[]{:S(2)}, u32[]{:S(2)}) async-start(f32[8,256,512]{1,2,0:T(8,128)} %stack.10), calls=%async_computation | async-start | bytes 8388608 | tf_op jit(solution)/shard_map/all_to_all | solution.py:29
  24.4 47.1 %all-to-all-done = f32[8,256,512]{1,2,0:T(8,128)} async-done(((f32[8,256,512]{1,2,0:T(8,128)}), f32[8,256,512]{1,2,0:T(8,128)}, u32[]{:S(2)}, u32[]{:S(2)}) %all-to-all-start) | async-done | bytes 4194336 | tf_op jit(solution)/shard_map/all_to_all | solution.py:29
  71.6 14.6 %all-gather.6.cloned.1.call-done = f32[4096,512]{1,0:T(8,128)} async-done(((f32[256,512]{1,0:T(8,128)}), f32[4096,512]{1,0:T(8,128)}) %all-gather.6.cloned.1.call-update) | async-done | bytes 8388624 | tf_op jit(solution)/shard_map/all_gather | solution.py:33
  86.1 17.7 %fusion = f32[256,512]{1,0:T(8,128)} fusion(f32[256,512]{1,0:T(8,128)S(1)} %copy.35, f32[256,512]{1,0:T(8,128)S(1)} %copy-done.2, pred[]{:T(512)} %bitcast.4, f32[256,4096]{0,1:T(8,128)} %bitcast.10, f32[4096,512]{1,0:T(8,128)} %all-gather.6.cloned.1.call-done), kind=kOutput, calls=%fused_computation.7 | convolution fusion | flops 6442975232 | bytes 14155777 | tf_op jit(solution)/shard_map/dot_general | solution.py:31
  105.1 2.3 stack.11
  107.4 5.3 %all-to-all-start.1 = ((f32[8,256,512]{1,2,0:T(8,128)}), f32[8,256,512]{1,2,0:T(8,128)}, u32[]{:S(2)}, u32[]{:S(2)}) async-start(f32[8,256,512]{1,2,0:T(8,128)} %stack.11), calls=%async_computation.1 | async-start | bytes 8388608 | tf_op jit(solution)/shard_map/all_to_all | solution.py:29
  114.1 47.5 %all-to-all-done.1 = f32[8,256,512]{1,2,0:T(8,128)} async-done(((f32[8,256,512]{1,2,0:T(8,128)}), f32[8,256,512]{1,2,0:T(8,128)}, u32[]{:S(2)}, u32[]{:S(2)}) %all-to-all-start.1) | async-done | bytes 4194336 | tf_op jit(solution)/shard_map/all_to_all | solution.py:29
  161.6 12.7 %all-gather.8.cloned.1.call-done = f32[4096,512]{1,0:T(8,128)} async-done(((f32[256,512]{1,0:T(8,128)}), f32[4096,512]{1,0:T(8,128)}) %all-gather.8.cloned.1.call-update) | async-done | bytes 8388624 | tf_op jit(solution)/shard_map/all_gather | solution.py:33
  174.4 17.7 %fusion.1 = f32[256,512]{1,0:T(8,128)} fusion(f32[256,512]{1,0:T(8,128)S(1)} %copy.38, f32[256,512]{1,0:T(8,128)S(1)} %copy-done.4, pred[]{:T(512)} %bitcast.3, f32[256,4096]{0,1:T(8,128)} %bitcast.14, f32[4096,512]{1,0:T(8,128)} %all-gather.8.cloned.1.call-done), kind=kOutput, calls=%fused_computation.8 | convolution fusion | flops 6442975232 | bytes 14155777 | tf_op jit(solution)/shard_map/dot_general | solution.py:31
  193.3 2.3 stack.12
  195.6 5.3 %all-to-all-start.2 = ((f32[8,256,512]{1,2,0:T(8,128)}), f32[8,256,512]{1,2,0:T(8,128)}, u32[]{:S(2)}, u32[]{:S(2)}) async-start(f32[8,256,512]{1,2,0:T(8,128)} %stack.12), calls=%async_computation.2 | async-start | bytes 8388608 | tf_op jit(solution)/shard_map/all_to_all | solution.py:29
  202.6 47.2 %all-to-all-done.2 = f32[8,256,512]{1,2,0:T(8,128)} async-done(((f32[8,256,512]{1,2,0:T(8,128)}), f32[8,256,512]{1,2,0:T(8,128)}, u32[]{:S(2)}, u32[]{:S(2)}) %all-to-all-start.2) | async-done | bytes 4194336 | tf_op jit(solution)/shard_map/all_to_all | solution.py:29
  249.8 12.7 %all-gather.10.cloned.1.call-done = f32[4096,512]{1,0:T(8,128)} async-done(((f32[256,512]{1,0:T(8,128)}), f32[4096,512]{1,0:T(8,128)}) %all-gather.10.cloned.1.call-update) | async-done | bytes 8388624 | tf_op jit(solution)/shard_map/all_gather | solution.py:33
  262.6 17.7 %fusion.2 = f32[256,512]{1,0:T(8,128)} fusion(f32[256,512]{1,0:T(8,128)S(1)} %copy.41, f32[256,512]{1,0:T(8,128)S(1)} %copy-done.5, pred[]{:T(512)} %bitcast.2, f32[256,4096]{0,1:T(8,128)} %bitcast.18, f32[4096,512]{1,0:T(8,128)} %all-gather.10.cloned.1.call-done), kind=kOutput, calls=%fused_computation.9 | convolution fusion | flops 6442975232 | bytes 14155777 | tf_op jit(solution)/shard_map/dot_general | solution.py:31
  281.5 2.3 stack.13
  283.8 5.3 %all-to-all-start.3 = ((f32[8,256,512]{1,2,0:T(8,128)}), f32[8,256,512]{1,2,0:T(8,128)}, u32[]{:S(2)}, u32[]{:S(2)}) async-start(f32[8,256,512]{1,2,0:T(8,128)} %stack.13), calls=%async_computation.3 | async-start | bytes 8388608 | tf_op jit(solution)/shard_map/all_to_all | solution.py:29
  290.3 47.7 %all-to-all-done.3 = f32[8,256,512]{1,2,0:T(8,128)} async-done(((f32[8,256,512]{1,2,0:T(8,128)}), f32[8,256,512]{1,2,0:T(8,128)}, u32[]{:S(2)}, u32[]{:S(2)}) %all-to-all-start.3) | async-done | bytes 4194336 | tf_op jit(solution)/shard_map/all_to_all | solution.py:29
  338.0 12.7 %all-gather.12.cloned.1.call-done = f32[4096,512]{1,0:T(8,128)} async-done(((f32[256,512]{1,0:T(8,128)}), f32[4096,512]{1,0:T(8,128)}) %all-gather.12.cloned.1.call-update) | async-done | bytes 8388624 | tf_op jit(solution)/shard_map/all_gather | solution.py:33
  350.8 17.7 %fusion.3 = f32[256,512]{1,0:T(8,128)} fusion(f32[256,512]{1,0:T(8,128)S(1)} %copy.44, f32[256,512]{1,0:T(8,128)S(1)} %copy-done.6, pred[]{:T(512)} %bitcast.1, f32[256,4096]{0,1:T(8,128)} %bitcast.22, f32[4096,512]{1,0:T(8,128)} %all-gather.12.cloned.1.call-done), kind=kOutput, calls=%fused_computation.10 | convolution fusion | flops 6442975232 | bytes 14155777 | tf_op jit(solution)/shard_map/dot_general | solution.py:31
  372.0 5.5 %all-to-all-start.4 = ((f32[8,256,512]{1,2,0:T(8,128)}), f32[8,256,512]{1,2,0:T(8,128)}, u32[]{:S(2)}, u32[]{:S(2)}) async-start(f32[8,256,512]{1,2,0:T(8,128)} %stack.14), calls=%async_computation.4 | async-start | bytes 8388608 | tf_op jit(solution)/shard_map/all_to_all | solution.py:29
  378.7 47.8 %all-to-all-done.4 = f32[8,256,512]{1,2,0:T(8,128)} async-done(((f32[8,256,512]{1,2,0:T(8,128)}), f32[8,256,512]{1,2,0:T(8,128)}, u32[]{:S(2)}, u32[]{:S(2)}) %all-to-all-start.4) | async-done | bytes 4194336 | tf_op jit(solution)/shard_map/all_to_all | solution.py:29
  426.4 12.5 %all-gather.14.cloned.1.call-done = f32[4096,512]{1,0:T(8,128)} async-done(((f32[256,512]{1,0:T(8,128)}), f32[4096,512]{1,0:T(8,128)}) %all-gather.14.cloned.1.call-update) | async-done | bytes 8388624 | tf_op jit(solution)/shard_map/all_gather | solution.py:33
  439.0 17.7 %fusion.4 = f32[256,512]{1,0:T(8,128)} fusion(f32[256,512]{1,0:T(8,128)S(1)} %copy.47, f32[256,512]{1,0:T(8,128)S(1)} %copy-done.3, pred[]{:T(512)} %bitcast, f32[256,4096]{0,1:T(8,128)} %bitcast.26, f32[4096,512]{1,0:T(8,128)} %all-gather.14.cloned.1.call-done), kind=kOutput, calls=%fused_computation.11 | convolution fusion | flops 6442975232 | bytes 14155777 | tf_op jit(solution)/shard_map/dot_general | solution.py:31
  (75 shorter events, 18.2 us)
Async XLA Ops:
  6.5 0.9 copy-start
  6.5 79.6 %all-gather.6.cloned.1.call-start = ((), (), s32[]{:S(2)}) async-start(), calls=%async_computation.5 | async-start | bytes 8912896 | tf_op jit(solution)/shard_map/all_gather | solution.py:33
  15.7 7.4 %copy-start.7 = (s32[5]{0:T(128)S(1)}, s32[5]{0:T(128)}, u32[]{:S(2)}) copy-start(s32[5]{0:T(128)} %param.6) | copy-start | bytes 64
  15.7 70.4 %copy-start.2 = (f32[256,512]{1,0:T(8,128)S(1)}, f32[256,512]{1,0:T(8,128)}, u32[]{:S(2)}) copy-start(f32[256,512]{1,0:T(8,128)} %mul.45) | copy-start | bytes 1572868
  15.7 55.9 %all-to-all-start = ((f32[8,256,512]{1,2,0:T(8,128)}), f32[8,256,512]{1,2,0:T(8,128)}, u32[]{:S(2)}, u32[]{:S(2)}) async-start(f32[8,256,512]{1,2,0:T(8,128)} %stack.10), calls=%async_computation | async-start | bytes 8388608 | tf_op jit(solution)/shard_map/all_to_all | solution.py:29
  22.6 151.7 %all-gather.8.cloned.1.call-start = ((), (), s32[]{:S(2)}) async-start(), calls=%async_computation.6 | async-start | bytes 8912896 | tf_op jit(solution)/shard_map/all_gather | solution.py:33
  107.4 66.9 %copy-start.4 = (f32[256,512]{1,0:T(8,128)S(1)}, f32[256,512]{1,0:T(8,128)}, u32[]{:S(2)}) copy-start(f32[256,512]{1,0:T(8,128)} %fusion) | copy-start | bytes 1572868
  107.4 54.2 %all-to-all-start.1 = ((f32[8,256,512]{1,2,0:T(8,128)}), f32[8,256,512]{1,2,0:T(8,128)}, u32[]{:S(2)}, u32[]{:S(2)}) async-start(f32[8,256,512]{1,2,0:T(8,128)} %stack.11), calls=%async_computation.1 | async-start | bytes 8388608 | tf_op jit(solution)/shard_map/all_to_all | solution.py:29
  112.7 149.9 %all-gather.10.cloned.1.call-start = ((), (), s32[]{:S(2)}) async-start(), calls=%async_computation.7 | async-start | bytes 8912896 | tf_op jit(solution)/shard_map/all_gather | solution.py:33
  195.6 66.9 %copy-start.5 = (f32[256,512]{1,0:T(8,128)S(1)}, f32[256,512]{1,0:T(8,128)}, u32[]{:S(2)}) copy-start(f32[256,512]{1,0:T(8,128)} %fusion.1) | copy-start | bytes 1572868
  195.6 54.2 %all-to-all-start.2 = ((f32[8,256,512]{1,2,0:T(8,128)}), f32[8,256,512]{1,2,0:T(8,128)}, u32[]{:S(2)}, u32[]{:S(2)}) async-start(f32[8,256,512]{1,2,0:T(8,128)} %stack.12), calls=%async_computation.2 | async-start | bytes 8388608 | tf_op jit(solution)/shard_map/all_to_all | solution.py:29
  200.9 149.9 %all-gather.12.cloned.1.call-start = ((), (), s32[]{:S(2)}) async-start(), calls=%async_computation.8 | async-start | bytes 8912896 | tf_op jit(solution)/shard_map/all_gather | solution.py:33
  283.8 66.9 %copy-start.6 = (f32[256,512]{1,0:T(8,128)S(1)}, f32[256,512]{1,0:T(8,128)}, u32[]{:S(2)}) copy-start(f32[256,512]{1,0:T(8,128)} %fusion.2) | copy-start | bytes 1572868
  283.8 54.2 %all-to-all-start.3 = ((f32[8,256,512]{1,2,0:T(8,128)}), f32[8,256,512]{1,2,0:T(8,128)}, u32[]{:S(2)}, u32[]{:S(2)}) async-start(f32[8,256,512]{1,2,0:T(8,128)} %stack.13), calls=%async_computation.3 | async-start | bytes 8388608 | tf_op jit(solution)/shard_map/all_to_all | solution.py:29
  289.1 149.9 %all-gather.14.cloned.1.call-start = ((), (), s32[]{:S(2)}) async-start(), calls=%async_computation.9 | async-start | bytes 8912896 | tf_op jit(solution)/shard_map/all_gather | solution.py:33
  372.0 66.9 %copy-start.3 = (f32[256,512]{1,0:T(8,128)S(1)}, f32[256,512]{1,0:T(8,128)}, u32[]{:S(2)}) copy-start(f32[256,512]{1,0:T(8,128)} %fusion.3) | copy-start | bytes 1572868
  372.0 54.4 %all-to-all-start.4 = ((f32[8,256,512]{1,2,0:T(8,128)}), f32[8,256,512]{1,2,0:T(8,128)}, u32[]{:S(2)}, u32[]{:S(2)}) async-start(f32[8,256,512]{1,2,0:T(8,128)} %stack.14), calls=%async_computation.4 | async-start | bytes 8388608 | tf_op jit(solution)/shard_map/all_to_all | solution.py:29
  439.0 17.7 %copy-start.1 = (s32[6,64,64]{2,1,0:T(8,128)S(1)}, s32[6,64,64]{2,1,0:T(8,128)}, u32[]{:S(2)}) copy-start(s32[6,64,64]{2,1,0:T(8,128)} %param.5) | copy-start | bytes 294916
Sparse Core Ops, SparseCore 0:
  12.3 73.8 all-gather.5
  104.0 70.3 all-gather.7
  192.2 70.3 all-gather.9
  280.4 70.3 all-gather.11
  368.6 70.3 all-gather.13
